TPU v7x, 32 devices: a whole 2x2x4 slice. The times are simulated.
32 devices in a mesh: groups: 2 (over y), emit: 4 (over z), recv: 4 (over x, core).
Axes of the slice: x: 2, y: 2, z: 4, core: 2. Of those that a mesh axis runs over, the one named last changes fastest.
Arguments:
- positions: float32 [3, 8192], P(None, ('groups', 'emit', 'recv')), parts along dimension 1, may hold values from 0 to 1
- angles: float32 [2, 8192], P(None, ('groups', 'emit', 'recv')), parts along dimension 1, may hold values from -3.140625 to 3.140625
- areas: float32 [8192], P(('groups', 'emit', 'recv')), parts along dimension 0, may hold values from 0.00024414062 to 0.00390625
- emissivity: float32 [8192], P(('groups', 'emit', 'recv')), parts along dimension 0, may hold values from 0.1 to 0.9
- emission: float32 [32, 8192], P(None, ('groups', 'emit', 'recv')), parts along dimension 1, may hold values from 0.5 to 2
- radiosity_in: float32 [32, 8192], P(None, ('groups', 'emit', 'recv')), parts along dimension 1, may hold values from 0.2 to 2
- adjoint_in: float32 [32, 8192], P(None, ('groups', 'emit', 'recv')), parts along dimension 1, may hold values from 0 to 1.5
- visibility: int32 [64, 32], P(('groups', 'emit')), parts along dimension 0, may hold values 0 or 1
- inlet_patches: int32 [4096], P('groups'), parts along dimension 0, may hold values from 0 to 4095
- inlet_weights: float32 [32, 4096], P(None, 'groups'), parts along dimension 1, may hold values from 0.5 to 2
Outputs:
- radiosity_out: float32 [32, 8192], P(None, ('groups', 'emit', 'recv')), parts along dimension 1
- adjoint_out: float32 [32, 8192], P(None, ('groups', 'emit', 'recv')), parts along dimension 1
- emissivity_grad: float32 [8192], P(('groups', 'emit', 'recv')), parts along dimension 0
There are 2 independent parts, one for each index of `groups`. A program takes and returns all parts, laid end to end along the dimension named above; each array names one. Nothing has to cross between parts.
Inputs may be any that keep to these rules, and one draw needn't show every extreme that they name: `inlet_patches`: an inlet patch may be listed more than once.
All inputs are finite; a program needn't handle non-finite values. No bound on the sum of `visibility` on one device may be relied on, other than what follows from the above.
Results may differ from a plain program's by a relative error of at most 0.0003.
Values may be sent and summed in bfloat16 or wider, within the bound.
No kernel may reach another device: no remote copies, remote signals or barrier semaphores. Data moves between devices by JAX's collectives and lax.ppermute only.
A program may use at most 64 MiB of HBM per device.

v0:
```python
import math
import jax
import jax.numpy as jnp
from jax import lax
from jax.sharding import PartitionSpec as P

BLK = 128


def patch_geometry(positions, angles, areas):
    polar = angles[0]
    azimuth = angles[1]
    normal = jnp.stack(
        [jnp.sin(polar) * jnp.cos(azimuth), jnp.sin(polar) * jnp.sin(azimuth), jnp.cos(polar)]
    )
    return jnp.concatenate([positions, normal, areas[None, :]], axis=0)


def view_tile(row_geom, col_geom, block_mask):
    delta_x = col_geom[0][None, :] - row_geom[0][:, None]
    delta_y = col_geom[1][None, :] - row_geom[1][:, None]
    delta_z = col_geom[2][None, :] - row_geom[2][:, None]
    dist_sq = delta_x * delta_x + delta_y * delta_y + delta_z * delta_z
    cos_emit = jnp.maximum(
        row_geom[3][:, None] * delta_x
        + row_geom[4][:, None] * delta_y
        + row_geom[5][:, None] * delta_z,
        0.0,
    )
    cos_recv = jnp.maximum(
        -(
            col_geom[3][None, :] * delta_x
            + col_geom[4][None, :] * delta_y
            + col_geom[5][None, :] * delta_z
        ),
        0.0,
    )
    patch_area = row_geom[6][:, None]
    spread = dist_sq + patch_area
    kernel = cos_emit * cos_recv * patch_area / (math.pi * spread * spread)
    row_blocks, col_blocks = block_mask.shape
    rows_total = row_geom.shape[1]
    cols_total = col_geom.shape[1]
    expanded = jnp.broadcast_to(
        block_mask[:, None, :, None],
        (row_blocks, rows_total // row_blocks, col_blocks, cols_total // col_blocks),
    ).reshape(rows_total, cols_total)
    return (expanded * kernel).astype(jnp.bfloat16)


def block_width():
    return 128


def local(
    positions,
    angles,
    areas,
    emissivity,
    emission,
    radiosity_in,
    adjoint_in,
    visibility,
    inlet_patches,
    inlet_weights,
):
    emit_count = lax.axis_size("emit")
    recv_count = lax.axis_size("recv")
    emit_index = lax.axis_index("emit")
    recv_index = lax.axis_index("recv")
    own_count = areas.shape[0]
    cases = emission.shape[0]
    geometry = patch_geometry(positions, angles, areas)
    reflect = 1.0 - emissivity
    own_weights = (reflect[None, :] * adjoint_in).astype(jnp.bfloat16)
    own_values = radiosity_in.astype(jnp.bfloat16)
    mask_rows = visibility.shape[0]
    per_block = visibility.shape[1] // emit_count
    own_blocks = own_count // BLK
    folded_mask = visibility.astype(jnp.float32).reshape(mask_rows, emit_count, per_block)
    tile_mask = lax.dynamic_slice_in_dim(
        folded_mask, recv_index * own_blocks, own_blocks, 2
    ).reshape(mask_rows, emit_count * own_blocks)
    row_total = own_count * recv_count
    col_total = own_count * emit_count
    row_values = lax.all_gather(own_values, "recv", axis=1, tiled=True)
    col_weight = lax.all_gather(own_weights, "emit", axis=1, tiled=True)
    start_state = (
        jnp.zeros((cases, col_total), jnp.float32),
        jnp.zeros((cases, row_total), jnp.float32),
    )
    col_geom = lax.all_gather(geometry, "emit", axis=1, tiled=True)
    geom_piece = lax.all_gather(geometry, "recv", axis=1, tiled=True)
    count = geom_piece.shape[1]
    width = block_width()

    def inner(number, state):
        fwd_total, adj_total = state
        offset = number * width
        geom_part = lax.dynamic_slice_in_dim(geom_piece, offset, width, 1)
        value_part = lax.dynamic_slice_in_dim(row_values, offset, width, 1)
        mask_part = lax.dynamic_slice_in_dim(tile_mask, offset // BLK, width // BLK, 0)
        tile = view_tile(geom_part, col_geom, mask_part)
        fwd_total = fwd_total + jnp.dot(value_part, tile, preferred_element_type=jnp.float32)
        adj_part = lax.dot_general(
            col_weight, tile, (((1,), (1,)), ((), ())), preferred_element_type=jnp.float32
        )
        adj_total = lax.dynamic_update_slice_in_dim(adj_total, adj_part, offset, 1)
        return (fwd_total, adj_total)

    forward, adjoint = lax.fori_loop(0, count // width, inner, start_state)
    incoming = lax.psum_scatter(forward, "emit", scatter_dimension=1, tiled=True)
    returned = lax.psum_scatter(adjoint, "recv", scatter_dimension=1, tiled=True)
    own_ids = (emit_index * recv_count + recv_index) * own_count + lax.iota(jnp.int32, own_count)
    selector = (inlet_patches[:, None] == own_ids[None, :]).astype(jnp.float32)
    source = jnp.dot(
        inlet_weights, selector, precision=lax.Precision.HIGHEST, preferred_element_type=jnp.float32
    )
    radiosity_out = emissivity[None, :] * emission + reflect[None, :] * incoming
    adjoint_out = source + returned
    emissivity_grad = jnp.sum(adjoint_out * (emission - incoming), axis=0)
    return (radiosity_out, adjoint_out, emissivity_grad)


def solution(mesh):
    placed = (
        P(None, ("groups", "emit", "recv")),
        P(None, ("groups", "emit", "recv")),
        P(("groups", "emit", "recv")),
        P(("groups", "emit", "recv")),
        P(None, ("groups", "emit", "recv")),
        P(None, ("groups", "emit", "recv")),
        P(None, ("groups", "emit", "recv")),
        P(("groups", "emit"), None),
        P("groups"),
        P(None, "groups"),
    )
    return jax.shard_map(
        local,
        mesh=mesh,
        in_specs=placed,
        out_specs=(
            P(None, ("groups", "emit", "recv")),
            P(None, ("groups", "emit", "recv")),
            P(("groups", "emit", "recv")),
        ),
        check_vma=False,
    )
```

profile of v0, /device:TPU:0, one launch (start us, length us, event | category | flops | bytes accessed | tf_op | source)
XLA Modules:
  0.0 115.8 jit_solution(4974398801967030085)
XLA Ops:
  7.2 0.8 slice_cosine_fusion
  8.8 14.8 %all_gather.14 = f32[7,1024]{1,0:T(8,128)S(1)} all-gather(f32[7,256]{1,0:T(8,128)S(1)} %concatenate.3), channel_id=1, replica_groups=mesh['groups'=2,'emit'=4,'recv'=4] {'emit'}, dimensions={1}, use_global_device_ids=true | all-gather | bytes 35840 | tf_op jit(solution)/shard_map/all_gather | solution.py:92
  23.6 5.2 %all_gather.13 = f32[7,1024]{1,0:T(8,128)S(1)} all-gather(f32[7,256]{1,0:T(8,128)S(1)} %concatenate.3), channel_id=1, replica_groups=mesh['groups'=2,'emit'=4,'recv'=4] {'recv'}, dimensions={1}, use_global_device_ids=true | all-gather | bytes 35840 | tf_op jit(solution)/shard_map/all_gather | solution.py:93
  31.1 5.2 %all_gather.12 = bf16[32,1024]{1,0:T(8,128)(2,1)S(1)} all-gather(bf16[32,256]{1,0:T(8,128)(2,1)S(1)} %convert_element_type.20), channel_id=1, replica_groups=mesh['groups'=2,'emit'=4,'recv'=4] {'recv'}, dimensions={1}, use_global_device_ids=true | all-gather | bytes 81920 | tf_op jit(solution)/shard_map/all_gather | solution.py:86
  36.3 13.1 %all_gather.15 = bf16[32,1024]{1,0:T(8,128)(2,1)S(1)} all-gather(bf16[32,256]{1,0:T(8,128)(2,1)S(1)} %multiply_convert_fusion), channel_id=1, replica_groups=mesh['groups'=2,'emit'=4,'recv'=4] {'emit'}, dimensions={1}, use_global_device_ids=true | all-gather | bytes 81920 | tf_op jit(solution)/shard_map/all_gather | solution.py:87
  49.4 13.7 %while.18 = (s32[]{:T(128)}, f32[32,1024]{1,0:T(8,128)S(1)}, f32[32,1024]{1,0:T(8,128)S(1)}, bf16[32,1024]{1,0:T(8,128)(2,1)S(1)}, f32[8,8]{1,0:T(8,128)S(1)}, /...) while((s32[]{:T(128)}, f32[32,1024]{1,0:T(8,128)S(1)}, ...), condition=%wide.region_1.2_spmd.clone, body=%wide.region_0.1_spmd.clone.sunk | while | flops 24444952 | bytes 484852 | solution.py:111
  49.6 0.8 convolution_add_fusion.2
  50.4 0.8 fusion.47
  51.3 0.8 convolution_add_fusion.2
  52.1 0.8 fusion.47
  53.0 0.8 convolution_add_fusion.2
  54.7 0.8 convolution_add_fusion.2
  55.5 0.8 fusion.47
  56.4 0.8 convolution_add_fusion.2
  57.2 0.8 fusion.47
  58.1 0.8 convolution_add_fusion.2
  58.9 0.8 fusion.47
  59.8 0.8 convolution_add_fusion.2
  60.6 0.8 fusion.47
  61.5 0.8 convolution_add_fusion.2
  62.4 0.8 fusion.47
  64.6 20.0 %reduce-scatter.5.cloned.1.call-done = f32[32,256]{1,0:T(8,128)} async-done(((f32[32,1024]{1,0:T(8,128)}), f32[32,256]{1,0:T(8,128)}) %reduce-scatter.5.cloned.1.call-update) | async-done | bytes 32784 | tf_op jit(solution)/shard_map/reduce_scatter | solution.py:113
  84.6 21.6 %reduce-scatter.3.cloned.1.call-done = f32[32,256]{1,0:T(8,128)} async-done(((f32[32,1024]{1,0:T(8,128)}), f32[32,256]{1,0:T(8,128)}) %reduce-scatter.3.cloned.1.call-update) | async-done | bytes 32784 | tf_op jit(solution)/shard_map/reduce_scatter | solution.py:112
  106.2 2.8 %multiply_reduce_fusion = (f32[256]{0:T(256)}, f32[32,256]{1,0:T(8,128)}, f32[32,256]{1,0:T(8,128)}) fusion(f32[32,256]{1,0:T(8,128)S(1)} %copy-done.5, f32[32,256]{1,0:T(8,128)} %reduce-scatter.3.cloned.1.call-done, f32[256]{0:T(256)S(1)} %broadcast_subtract_fusion, f32[256]{0:T(256)S(1)} %copy-done.4, f32[32,256]{1,0:T(8,128)} %reduce-scatter.5.cloned.1.call-done, ...), kind=kOutput, calls=%fused_computation.47 | convolution fusion | flops 201907968 | bytes 438272 | tf_op jit(solution)/shard_map/dot_general | solution.py:116
  (70 shorter events, 6.1 us)
Async XLA Ops:
  7.2 99.0 %copy-start = (f32[32,2048]{1,0:T(8,128)S(1)}, f32[32,2048]{1,0:T(8,128)}, u32[]{:S(2)}) copy-start(f32[32,2048]{1,0:T(8,128)} %param.21) | copy-start | bytes 786436
  7.2 29.1 %copy-start.3 = (f32[32,256]{1,0:T(8,128)S(1)}, f32[32,256]{1,0:T(8,128)}, u32[]{:S(2)}) copy-start(f32[32,256]{1,0:T(8,128)} %param.18) | copy-start | bytes 98308
  7.2 77.4 %reduce-scatter.5.cloned.1.call-start = ((), (), s32[]{:S(2)}) async-start(), calls=%async_computation.3 | async-start | bytes 163840 | tf_op jit(solution)/shard_map/reduce_scatter | solution.py:113
  63.1 0.7 copy-start.1
  63.1 0.7 copy-start.2
  63.1 43.0 %copy-start.4 = (f32[256]{0:T(256)S(1)}, f32[256]{0:T(256)}, u32[]{:S(2)}) copy-start(f32[256]{0:T(256)} %param.15) | copy-start | bytes 3076
  63.2 43.0 %copy-start.5 = (f32[32,256]{1,0:T(8,128)S(1)}, f32[32,256]{1,0:T(8,128)}, u32[]{:S(2)}) copy-start(f32[32,256]{1,0:T(8,128)} %param.16) | copy-start | bytes 98308
  63.2 43.0 %copy-start.6 = (s32[2048]{0:T(1024)S(1)}, s32[2048]{0:T(1024)}, u32[]{:S(2)}) copy-start(s32[2048]{0:T(1024)} %param.20) | copy-start | bytes 24580
  63.8 42.3 %reduce-scatter.3.cloned.1.call-start = ((), (), s32[]{:S(2)}) async-start(), calls=%async_computation.2 | async-start | bytes 163840 | tf_op jit(solution)/shard_map/reduce_scatter | solution.py:112
Sparse Core Ops, SparseCore 0:
  63.9 20.5 reduce-scatter.4
  86.9 19.1 reduce-scatter.2
where the time goes:
time: 116 us
  waiting for transfers between devices  42.3 us (36%)
  blocking collectives  38.3 us (33%)
  matrix products  15.3 us (13%)
  between operations  14.1 us (12%)
  other arithmetic  2.97 us (3%)
  local copies, waits for them, and re-layouts  2.42 us (2%)
    reduce_scatter x1, waiting for transfers between devices, local(): lax.psum_scatter(forward, 'emit', scatter_dimension=1, tiled=True)  21.6 us
    reduce_scatter x1, waiting for transfers between devices, local(): lax.psum_scatter(adjoint, 'recv', scatter_dimension=1, tiled=True)  20 us
    all_gather x1, blocking collectives, local(): col_geom = lax.all_gather(geometry, 'emit', axis=1, tiled=True)  14.8 us
    all_gather x1, blocking collectives, local(): col_weight = lax.all_gather(own_weights, 'emit', axis=1, tiled=True)  13.1 us
    dot_general x8, matrix products, inner(): jnp.dot(value_part, tile, preferred_element_type=jnp.float32)  6.43 us
    dot_general x8, matrix products, inner(): lax.dot_general(col_weight, tile, (((1,), (1,)), ((), ())), preferred_ele...  6.15 us
    all_gather x1, blocking collectives, local(): row_values = lax.all_gather(own_values, 'recv', axis=1, tiled=True)  5.23 us
    all_gather x1, blocking collectives, local(): geom_piece = lax.all_gather(geometry, 'recv', axis=1, tiled=True)  5.18 us
  transfers between devices with their start and end apart: 2, of which 2 were waited for; matrix products, arithmetic and copies ran while one was open for 0% of the time, Pallas kernels for 0%

commit v1 on v0

--- a/solution.py
+++ b/solution.py
@@ -84,12 +84,17 @@
     row_total = own_count * recv_count
     col_total = own_count * emit_count
     row_values = lax.all_gather(own_values, "recv", axis=1, tiled=True)
-    col_weight = lax.all_gather(own_weights, "emit", axis=1, tiled=True)
     start_state = (
         jnp.zeros((cases, col_total), jnp.float32),
         jnp.zeros((cases, row_total), jnp.float32),
     )
-    col_geom = lax.all_gather(geometry, "emit", axis=1, tiled=True)
+    col_weight, col_geom = jnp.split(
+        lax.all_gather(
+            jnp.concatenate([own_weights, geometry], axis=0), "emit", axis=1, tiled=True
+        ),
+        [own_weights.shape[0]],
+        axis=0,
+    )
     geom_piece = lax.all_gather(geometry, "recv", axis=1, tiled=True)
     count = geom_piece.shape[1]
     width = block_width()

time: 116 us -> 104 us (0.90)
  blocking collectives: 38.3 us -> 25.6 us
    all_gather x2 -> x1, blocking collectives: 27.9 us -> 15.1 us  [local(): lax.all_gather(jnp.concatenate([own_weights, geometry], axis=0), 'emit',...]
where the time goes in v1:
time: 104 us
  waiting for transfers between devices  42.7 us (41%)
  blocking collectives  25.6 us (25%)
  matrix products  15.3 us (15%)
  between operations  14.2 us (14%)
  local copies, waits for them, and re-layouts  3.18 us (3%)
  other arithmetic  2.32 us (2%)
    reduce_scatter x1, waiting for transfers between devices, local(): lax.psum_scatter(forward, 'emit', scatter_dimension=1, tiled=True)  21.6 us
    reduce_scatter x1, waiting for transfers between devices, local(): lax.psum_scatter(adjoint, 'recv', scatter_dimension=1, tiled=True)  20.4 us
    all_gather x1, blocking collectives, local(): lax.all_gather(jnp.concatenate([own_weights, geometry], axis=0), 'emit',...  15.1 us
    dot_general x8, matrix products, inner(): jnp.dot(value_part, tile, preferred_element_type=jnp.float32)  6.43 us
    dot_general x8, matrix products, inner(): lax.dot_general(col_weight, tile, (((1,), (1,)), ((), ())), preferred_ele...  6.13 us
    all_gather x1, blocking collectives, local(): row_values = lax.all_gather(own_values, 'recv', axis=1, tiled=True)  5.23 us
    all_gather x1, blocking collectives, local(): geom_piece = lax.all_gather(geometry, 'recv', axis=1, tiled=True)  5.18 us
    dot_general x1, matrix products, local(): jnp.dot(inlet_weights, selector, precision=lax.Precision.HIGHEST, preferr...  2.76 us
  transfers between devices with their start and end apart: 2, of which 2 were waited for; matrix products, arithmetic and copies ran while one was open for 0% of the time, Pallas kernels for 0%

profile of v1, /device:TPU:0, one launch (start us, length us, event | category | flops | bytes accessed | tf_op | source)
XLA Modules:
  0.0 103.6 jit_solution(11484197688859641369)
XLA Ops:
  7.9 0.8 slice_cosine_fusion
  8.8 0.8 fusion.31
  11.0 15.1 %all_gather.11 = f32[39,1024]{1,0:T(8,128)S(1)} all-gather(f32[39,256]{1,0:T(8,128)S(1)} %concatenate.8), channel_id=1, replica_groups=mesh['groups'=2,'emit'=4,'recv'=4] {'emit'}, dimensions={1}, use_global_device_ids=true | all-gather | bytes 199680 | tf_op jit(solution)/shard_map/all_gather | solution.py:92
  26.4 5.2 %all_gather.10 = f32[7,1024]{1,0:T(8,128)S(1)} all-gather(f32[7,256]{1,0:T(8,128)S(1)} %concatenate.7), channel_id=1, replica_groups=mesh['groups'=2,'emit'=4,'recv'=4] {'recv'}, dimensions={1}, use_global_device_ids=true | all-gather | bytes 35840 | tf_op jit(solution)/shard_map/all_gather | solution.py:98
  31.5 5.2 %all_gather.9 = bf16[32,1024]{1,0:T(8,128)(2,1)S(1)} all-gather(bf16[32,256]{1,0:T(8,128)(2,1)S(1)} %convert_element_type.23), channel_id=1, replica_groups=mesh['groups'=2,'emit'=4,'recv'=4] {'recv'}, dimensions={1}, use_global_device_ids=true | all-gather | bytes 81920 | tf_op jit(solution)/shard_map/all_gather | solution.py:86
  36.8 13.7 %while.18 = (s32[]{:T(128)}, f32[32,1024]{1,0:T(8,128)S(1)}, f32[32,1024]{1,0:T(8,128)S(1)}, bf16[32,1024]{1,0:T(8,128)(2,1)S(1)}, f32[8,8]{1,0:T(8,128)S(1)}, /...) while((s32[]{:T(128)}, f32[32,1024]{1,0:T(8,128)S(1)}, ...), condition=%wide.region_1.2_spmd.clone, body=%wide.region_0.1_spmd.clone.sunk | while | flops 24444952 | bytes 484852 | solution.py:116
  36.9 0.8 convolution_add_fusion.2
  37.8 0.8 fusion.48
  38.7 0.8 convolution_add_fusion.2
  39.5 0.8 fusion.48
  40.4 0.8 convolution_add_fusion.2
  41.2 0.8 fusion.48
  42.1 0.8 convolution_add_fusion.2
  42.9 0.8 fusion.48
  43.8 0.8 convolution_add_fusion.2
  44.6 0.8 fusion.48
  45.5 0.8 convolution_add_fusion.2
  46.3 0.8 fusion.48
  47.2 0.8 convolution_add_fusion.2
  48.0 0.8 fusion.48
  48.9 0.8 convolution_add_fusion.2
  51.9 20.4 %reduce-scatter.5.cloned.1.call-done = f32[32,256]{1,0:T(8,128)} async-done(((f32[32,1024]{1,0:T(8,128)}), f32[32,256]{1,0:T(8,128)}) %reduce-scatter.5.cloned.1.call-update) | async-done | bytes 32784 | tf_op jit(solution)/shard_map/reduce_scatter | solution.py:118
  72.4 21.6 %reduce-scatter.3.cloned.1.call-done = f32[32,256]{1,0:T(8,128)} async-done(((f32[32,1024]{1,0:T(8,128)}), f32[32,256]{1,0:T(8,128)}) %reduce-scatter.3.cloned.1.call-update) | async-done | bytes 32784 | tf_op jit(solution)/shard_map/reduce_scatter | solution.py:117
  94.0 2.8 %multiply_reduce_fusion = (f32[256]{0:T(256)}, f32[32,256]{1,0:T(8,128)}, f32[32,256]{1,0:T(8,128)}) fusion(f32[32,256]{1,0:T(8,128)S(1)} %copy-done.6, f32[32,256]{1,0:T(8,128)} %reduce-scatter.3.cloned.1.call-done, f32[256]{0:T(256)S(1)} %broadcast_subtract_fusion, f32[256]{0:T(256)S(1)} %copy-done.5, f32[32,256]{1,0:T(8,128)} %reduce-scatter.5.cloned.1.call-done, ...), kind=kOutput, calls=%fused_computation.47 | convolution fusion | flops 201907968 | bytes 438272 | tf_op jit(solution)/shard_map/dot_general | solution.py:121
  (74 shorter events, 5.5 us)
Async XLA Ops:
  7.2 86.8 %copy-start = (f32[32,2048]{1,0:T(8,128)S(1)}, f32[32,2048]{1,0:T(8,128)}, u32[]{:S(2)}) copy-start(f32[32,2048]{1,0:T(8,128)} %param.21) | copy-start | bytes 786436
  7.2 65.2 %reduce-scatter.5.cloned.1.call-start = ((), (), s32[]{:S(2)}) async-start(), calls=%async_computation.3 | async-start | bytes 163840 | tf_op jit(solution)/shard_map/reduce_scatter | solution.py:118
  9.5 16.6 %copy-start.4 = (s32[8,32]{1,0:T(8,128)S(1)}, s32[8,32]{1,0:T(8,128)}, u32[]{:S(2)}) copy-start(s32[8,32]{1,0:T(8,128)} %param.19) | copy-start | bytes 3076
  10.3 16.1 %copy-start.3 = (f32[32,256]{1,0:T(8,128)S(1)}, f32[32,256]{1,0:T(8,128)}, u32[]{:S(2)}) copy-start(f32[32,256]{1,0:T(8,128)} %param.17) | copy-start | bytes 98308
  50.5 0.7 copy-start.1
  50.5 0.7 copy-start.2
  50.5 43.5 %copy-start.5 = (f32[256]{0:T(256)S(1)}, f32[256]{0:T(256)}, u32[]{:S(2)}) copy-start(f32[256]{0:T(256)} %param.15) | copy-start | bytes 3076
  50.5 43.5 %copy-start.6 = (f32[32,256]{1,0:T(8,128)S(1)}, f32[32,256]{1,0:T(8,128)}, u32[]{:S(2)}) copy-start(f32[32,256]{1,0:T(8,128)} %param.16) | copy-start | bytes 98308
  50.5 43.5 %copy-start.7 = (s32[2048]{0:T(1024)S(1)}, s32[2048]{0:T(1024)}, u32[]{:S(2)}) copy-start(s32[2048]{0:T(1024)} %param.20) | copy-start | bytes 24580
  51.2 42.8 %reduce-scatter.3.cloned.1.call-start = ((), (), s32[]{:S(2)}) async-start(), calls=%async_computation.2 | async-start | bytes 163840 | tf_op jit(solution)/shard_map/reduce_scatter | solution.py:117
Sparse Core Ops, SparseCore 0:
  51.3 21.0 reduce-scatter.4
  74.7 19.2 reduce-scatter.2
